TPU v7x, 32 devices: a whole 2x2x4 slice. The times are simulated.
32 devices in a mesh: layer: 4 (over y, x), row: 2 (over core), col: 4 (over z).
Axes of the slice: x: 2, y: 2, z: 4, core: 2. Of those that a mesh axis runs over, the one named last changes fastest.
Arguments:
- cols: int32 [64, 16], P(('row', 'col'), 'layer'), may hold values from -1 to 63, as said below
- vals: bfloat16 [64, 16, 256, 256], P(('row', 'col'), 'layer'), as said below
- outcols: int32 [64, 4], P(('row', 'col')), may hold values from -1 to 63, as said below
Outputs:
- purified: bfloat16 [64, 4, 256, 256], P(('row', 'col'), 'layer')
Inputs may be any that keep to these rules, and one draw needn't show every extreme that they name: `cols`: slots 4 * l to 4 * l + 3 of block row i hold distinct block columns k with k mod 4 = l and |k - i| <= 6, or -1. Column i is always listed in row i, and k is listed in row i exactly when i is listed in row k. vals[i, s] is block (i, cols[i, s]) of a symmetric matrix: the block listed at (k, i) is the transpose of the one at (i, k). Slots holding -1 hold zeros. `outcols`: block row i lists distinct block columns j with i <= j <= i + 12, always i itself, or -1.
All inputs are finite; a program needn't handle non-finite values.
Results may differ from a plain program's by a relative error of at most 0.0085.
Values may be sent and summed in bfloat16 or wider, within the bound.
A program may use at most 64 MiB of HBM per device.

v0:
```python
import jax
import jax.numpy as jnp
from jax import lax
from jax.sharding import PartitionSpec as P

W = 6


def passed_along(value, axis, by):
    peers = lax.axis_size(axis)
    pairs = [(i, i + by) for i in range(peers) if 0 <= i + by < peers]
    return lax.ppermute(value, axis, pairs)


def per_device(cols, vals, outcols):
    rows = vals.shape[0]
    need = 2 * W
    hops = -(-need // rows)
    blocks_list = [vals]
    column_list = [cols]
    send_blocks = vals
    send_cols = cols
    for hop in range(1, hops + 1):
        count = min(rows, need - (hop - 1) * rows)
        got_blocks, got_cols = passed_along(
            (send_blocks[:count], send_cols[:count]), ("row", "col"), -1
        )
        blocks_list.append(got_blocks)
        column_list.append(got_cols)
        send_blocks = got_blocks
        send_cols = got_cols
    extended = jnp.concatenate(blocks_list, axis=0)
    extended_cols = jnp.concatenate(column_list, axis=0)
    offset_rows = lax.axis_index(("row", "col")) * rows

    def one_row(inputs):
        left, left_cols, targets = inputs
        where = jnp.clip(targets - offset_rows, 0, extended_cols.shape[0] - 1)
        right = extended[where]
        right_cols = extended_cols[where]
        hits = (
            (left_cols[None, :, None] == right_cols[:, None, :]) & (left_cols[None, :, None] >= 0)
        ).astype(jnp.bfloat16)
        moved = jnp.einsum(
            "ost,otab->osab", hits, right, preferred_element_type=jnp.float32
        ).astype(jnp.bfloat16)
        product = jnp.einsum("sab,oscb->oac", left, moved, preferred_element_type=jnp.float32)
        owned = (left_cols[None, :] == targets[:, None]).astype(jnp.bfloat16)
        twice = 2.0 * jnp.einsum("os,sab->oab", owned, left, preferred_element_type=jnp.float32)
        return jnp.where(targets[:, None, None] >= 0, twice - product, jnp.float32(0.0))

    partials = lax.map(one_row, (vals, cols, outcols))
    total = lax.psum(partials.astype(jnp.bfloat16), "layer").astype(jnp.float32)
    share = outcols.shape[1] // lax.axis_size("layer")
    mine = lax.dynamic_slice_in_dim(total, lax.axis_index("layer") * share, share, 1)
    return mine.astype(jnp.bfloat16)


def solution(mesh):
    in_specs = (
        P(("row", "col"), "layer"),
        P(("row", "col"), "layer", None, None),
        P(("row", "col"), None),
    )
    out_specs = P(("row", "col"), "layer", None, None)
    return jax.shard_map(
        per_device, mesh=mesh, in_specs=in_specs, out_specs=out_specs, check_vma=False
    )
```

profile of v0, /device:TPU:0, one launch (start us, length us, event | category | flops | bytes accessed | tf_op | source)
XLA Modules:
  0.0 372.5 jit_solution(15405082629851489519)
XLA Ops:
  8.0 94.4 %collective-permute-done.2 = bf16[8,4,256,256]{3,2,1,0:T(8,128)(2,1)S(1)} collective-permute-done((bf16[8,4,256,256]{3,2,1,0:T(8,128)(2,1)}, bf16[8,4,256,256]{3,2,1,0:T(8,128)(2,1)S(1)}, u32[]{:S(2)}, u32[]{:S(2)}) %collective-permute-start.2) | collective-permute-done | bytes 4194336 | tf_op jit(solution)/shard_map/ppermute | solution.py:12
  102.4 2.0 copy-done
  108.6 46.2 %collective-permute-done = s32[8,4]{0,1:T(4,128)S(1)} collective-permute-done((s32[8,4]{0,1:T(4,128)S(1)}, s32[8,4]{0,1:T(4,128)S(1)}, u32[]{:S(2)}, u32[]{:S(2)}) %collective-permute-start) | collective-permute-done | bytes 160 | tf_op jit(solution)/shard_map/ppermute | solution.py:12
  156.1 4.2 %collective-permute-done.1 = s32[4,4]{0,1:T(4,128)S(1)} collective-permute-done((s32[4,4]{0,1:T(4,128)S(1)}, s32[4,4]{0,1:T(4,128)S(1)}, u32[]{:S(2)}, u32[]{:S(2)}) %collective-permute-start.1) | collective-permute-done | bytes 96 | tf_op jit(solution)/shard_map/ppermute | solution.py:12
  160.4 8.8 %pad_maximum_fusion = bf16[20,4,256,256]{3,2,1,0:T(8,128)(2,1)} fusion(bf16[4,4,256,256]{3,2,1,0:T(8,128)(2,1)S(1)} %collective-permute-done.3, bf16[8,4,256,256]{3,2,1,0:T(8,128)(2,1)} %copy-done, bf16[8,4,256,256]{3,2,1,0:T(8,128)(2,1)} %param.6), kind=kLoop, calls=%fused_computation.35 | loop fusion | flops 10485760 | bytes 20971520 | tf_op jit(solution)/shard_map/concatenate | solution.py:32
  169.2 90.0 %while.10 = (s32[]{:T(128)}, bf16[8,4,256,256]{3,2,1,0:T(8,128)(2,1)}, s32[8,4]{1,0:T(8,128)S(1)}, s32[8,4]{1,0:T(8,128)S(1)}, bf16[8,4,256,256]{3,2,1,0:T(8,128...) while((s32[]{:T(128)}, bf16[8,4,256,256]{3,2,1,0:T(8,128)(2,1)}, ...), condition=%wide.region_1.2_spmd, body=%wide.region_0.1_spmd.sunk | while | flops 548144256 | bytes 19403772 | solution.py:52
  169.2 4.7 %gather_fusion = bf16[4,4,256,256]{3,2,1,0:T(8,128)(2,1)S(1)} fusion(bf16[20,4,256,256]{3,2,1,0:T(8,128)(2,1)} %get-tuple-element.168, s32[1024]{0:T(1024)S(1)} %pad_clamp_fusion.2), kind=kCustom, calls=%fused_computation.1.clone.1 | custom fusion | bytes 4194320 | tf_op jit(solution)/shard_map/while/body/eval_jaxpr/gather | solution.py:39
  174.5 1.8 fusion.37
  180.5 4.7 %gather_fusion = bf16[4,4,256,256]{3,2,1,0:T(8,128)(2,1)S(1)} fusion(bf16[20,4,256,256]{3,2,1,0:T(8,128)(2,1)} %get-tuple-element.168, s32[1024]{0:T(1024)S(1)} %pad_clamp_fusion.2), kind=kCustom, calls=%fused_computation.1.clone.1 | custom fusion | bytes 4194320 | tf_op jit(solution)/shard_map/while/body/eval_jaxpr/gather | solution.py:39
  185.7 1.8 fusion.37
  191.7 4.7 %gather_fusion = bf16[4,4,256,256]{3,2,1,0:T(8,128)(2,1)S(1)} fusion(bf16[20,4,256,256]{3,2,1,0:T(8,128)(2,1)} %get-tuple-element.168, s32[1024]{0:T(1024)S(1)} %pad_clamp_fusion.2), kind=kCustom, calls=%fused_computation.1.clone.1 | custom fusion | bytes 4194320 | tf_op jit(solution)/shard_map/while/body/eval_jaxpr/gather | solution.py:39
  197.0 1.8 fusion.37
  203.0 4.7 %gather_fusion = bf16[4,4,256,256]{3,2,1,0:T(8,128)(2,1)S(1)} fusion(bf16[20,4,256,256]{3,2,1,0:T(8,128)(2,1)} %get-tuple-element.168, s32[1024]{0:T(1024)S(1)} %pad_clamp_fusion.2), kind=kCustom, calls=%fused_computation.1.clone.1 | custom fusion | bytes 4194320 | tf_op jit(solution)/shard_map/while/body/eval_jaxpr/gather | solution.py:39
  208.2 1.8 fusion.37
  214.2 4.7 %gather_fusion = bf16[4,4,256,256]{3,2,1,0:T(8,128)(2,1)S(1)} fusion(bf16[20,4,256,256]{3,2,1,0:T(8,128)(2,1)} %get-tuple-element.168, s32[1024]{0:T(1024)S(1)} %pad_clamp_fusion.2), kind=kCustom, calls=%fused_computation.1.clone.1 | custom fusion | bytes 4194320 | tf_op jit(solution)/shard_map/while/body/eval_jaxpr/gather | solution.py:39
  219.5 1.8 fusion.37
  225.5 4.7 %gather_fusion = bf16[4,4,256,256]{3,2,1,0:T(8,128)(2,1)S(1)} fusion(bf16[20,4,256,256]{3,2,1,0:T(8,128)(2,1)} %get-tuple-element.168, s32[1024]{0:T(1024)S(1)} %pad_clamp_fusion.2), kind=kCustom, calls=%fused_computation.1.clone.1 | custom fusion | bytes 4194320 | tf_op jit(solution)/shard_map/while/body/eval_jaxpr/gather | solution.py:39
  230.7 1.8 fusion.37
  236.8 4.7 %gather_fusion = bf16[4,4,256,256]{3,2,1,0:T(8,128)(2,1)S(1)} fusion(bf16[20,4,256,256]{3,2,1,0:T(8,128)(2,1)} %get-tuple-element.168, s32[1024]{0:T(1024)S(1)} %pad_clamp_fusion.2), kind=kCustom, calls=%fused_computation.1.clone.1 | custom fusion | bytes 4194320 | tf_op jit(solution)/shard_map/while/body/eval_jaxpr/gather | solution.py:39
  242.0 1.8 fusion.37
  248.0 4.7 %gather_fusion = bf16[4,4,256,256]{3,2,1,0:T(8,128)(2,1)S(1)} fusion(bf16[20,4,256,256]{3,2,1,0:T(8,128)(2,1)} %get-tuple-element.168, s32[1024]{0:T(1024)S(1)} %pad_clamp_fusion.2), kind=kCustom, calls=%fused_computation.1.clone.1 | custom fusion | bytes 4194320 | tf_op jit(solution)/shard_map/while/body/eval_jaxpr/gather | solution.py:39
  253.2 1.8 fusion.37
  259.2 104.2 %all-reduce.2.cloned.1.call-done = bf16[8,4,256,256]{3,2,1,0:T(8,128)(2,1)} async-done(((bf16[8,4,256,256]{3,2,1,0:T(8,128)(2,1)}), bf16[8,4,256,256]{3,2,1,0:T(8,128)(2,1)}) %all-reduce.2.cloned.1.call-update) | async-done | bytes 4194320 | tf_op jit(solution)/shard_map/psum | solution.py:53
  363.4 2.3 convert_convert_fusion
  (98 shorter events, 45.3 us)
Async XLA Ops:
  6.5 100.6 %copy-start.1 = (s32[8,4]{0,1:T(4,128)S(1)}, s32[8,4]{0,1:T(4,128)}, u32[]{:S(2)}) copy-start(s32[8,4]{0,1:T(4,128)} %param.5) | copy-start | bytes 388
  6.5 102.0 %copy-start.2 = (s32[8,4]{0,1:T(4,128)S(1)}, s32[8,4]{0,1:T(4,128)}, u32[]{:S(2)}) copy-start(s32[8,4]{0,1:T(4,128)} %param.7) | copy-start | bytes 388
  6.5 356.9 %all-reduce.2.cloned.1.call-start = ((), (), s32[]{:S(2)}) async-start(), calls=%async_computation | async-start | bytes 8388608 | tf_op jit(solution)/shard_map/psum | solution.py:53
  6.5 95.9 %collective-permute-start.2 = (bf16[8,4,256,256]{3,2,1,0:T(8,128)(2,1)}, bf16[8,4,256,256]{3,2,1,0:T(8,128)(2,1)S(1)}, u32[]{:S(2)}, u32[]{:S(2)}) collective-permute-start(bf16[8,4,256,256]{3,2,1,0:T(8,128)(2,1)} %param.6), channel_id=1, source_target_pairs={{1,0},{2,1},{3,2},{4,3},{5,4},{6,5},{7,6},{9,8},{10,9},{11,10},{12... | collective-permute-start | bytes 12582920 | tf_op jit(solution)/shard_map/ppermute | solution.py:12
  102.4 2.0 copy-start
  105.9 54.6 %collective-permute-start.3 = (bf16[4,4,256,256]{3,2,1,0:T(8,128)(2,1)}, bf16[4,4,256,256]{3,2,1,0:T(8,128)(2,1)S(1)}, u32[]{:S(2)}, u32[]{:S(2)}) collective-permute-start(bf16[4,4,256,256]{3,2,1,0:T(8,128)(2,1)} %slice.12), channel_id=1, source_target_pairs={{1,0},{2,1},{3,2},{4,3},{5,4},{6,5},{7,6},{9,8},{10,9},{11,10},{12... | collective-permute-start | bytes 6291464 | tf_op jit(solution)/shard_map/ppermute | solution.py:12
  107.2 47.6 %collective-permute-start = (s32[8,4]{0,1:T(4,128)S(1)}, s32[8,4]{0,1:T(4,128)S(1)}, u32[]{:S(2)}, u32[]{:S(2)}) collective-permute-start(s32[8,4]{0,1:T(4,128)S(1)} %copy-done.1), channel_id=1, source_target_pairs={{1,0},{2,1},{3,2},{4,3},{5,4},{6,5},{7,6},{9,8},{10,9},{11,10},{12... | collective-permute-start | bytes 392 | tf_op jit(solution)/shard_map/ppermute | solution.py:12
  154.8 5.5 %collective-permute-start.1 = (s32[4,4]{0,1:T(4,128)S(1)}, s32[4,4]{0,1:T(4,128)S(1)}, u32[]{:S(2)}, u32[]{:S(2)}) collective-permute-start(s32[4,4]{0,1:T(4,128)S(1)} %bitcast.54), channel_id=1, source_target_pairs={{1,0},{2,1},{3,2},{4,3},{5,4},{6,5},{7,6},{9,8},{10,9},{11,10},{12... | collective-permute-start | bytes 200 | tf_op jit(solution)/shard_map/ppermute | solution.py:12
Sparse Core Ops, SparseCore 0:
  259.4 103.9 all-reduce.1
where the time goes:
time: 374 us; the launch traced here: 373 us
  waiting for transfers between devices  249 us (67%)
  local copies, waits for them, and re-layouts  67.6 us (18%)
  matrix products  25.5 us (7%)
  between operations  13.5 us (4%)
  other arithmetic  11.3 us (3%)
  starting transfers between devices  5.27 us (1%)
    ppermute x4, waiting for transfers between devices, passed_along(): return lax.ppermute(value, axis, pairs)  145 us
    psum x1, waiting for transfers between devices, per_device(): total = lax.psum(partials.astype(jnp.bfloat16), 'layer').astype(jnp.float32)  104 us
    gather x8, local copies, waits for them, and re-layouts, one_row(): right = extended[where]  37.3 us
    dot_general x8, matrix products, one_row(): jnp.einsum('ost,otab->osab', hits, right, preferred_element_type=jnp.floa...  14.1 us
    dynamic_slice x16, local copies, waits for them, and re-layouts, per_device(): partials = lax.map(one_row, (vals, cols, outcols))  11.9 us
    concatenate x1, other arithmetic, per_device(): extended = jnp.concatenate(blocks_list, axis=0)  8.76 us
  transfers between devices with their start and end apart: 5, of which 4 were waited for; matrix products, arithmetic and copies ran while one was open for 0% of the time, Pallas kernels for 0%

commit v1 on v0

v1 whole, which is shorter than its diff:
```python
import functools

import jax
import jax.numpy as jnp
from jax import lax
from jax.experimental import pallas as pl
from jax.experimental.pallas import tpu as pltpu
from jax.sharding import PartitionSpec as P

W = 6
MESH = pl.DeviceIdType.MESH


def kernel(
    sizes, cols_ref, targets_ref, vals_ref, out_ref,
    pack, halo, right, part, own, recv,
    halo_send, halo_recv, part_send, part_recv,
):
    rows, slots, outs, layers, groups, fine = sizes
    far = 2 * W
    steps = -(-(rows + W) // layers)
    layer = lax.axis_index("layer")
    group = lax.axis_index("row") * fine + lax.axis_index("col")
    base = group * rows
    zero_at = rows * slots
    halo_at = zero_at + 1

    def group_id(by):
        other = (group + by + groups) % groups
        return {"row": other // fine, "col": other % fine}

    def layer_id(by):
        return {"layer": (layer + by) % layers}

    def find(row, column):
        slot = jnp.int32(0)
        hit = jnp.int32(0)
        for s in range(slots):
            same = (cols_ref[row, s] == column).astype(jnp.int32)
            slot = slot + s * same
            hit = hit + same
        return jnp.minimum(slot, slots - 1), hit

    def halo_count(q):
        count = jnp.clip(q * layers + layer - rows + W + 1, 0, far)
        return jnp.where(q * layers + layer < rows + W, count, 0)

    def halo_copy(q, t, by):
        at = q * far + t
        return pltpu.make_async_remote_copy(
            src_ref=pack.at[at], dst_ref=halo.at[at],
            send_sem=halo_send.at[at], recv_sem=halo_recv.at[at],
            device_id=group_id(-by), device_id_type=MESH,
        )

    def part_copy(row, r):
        at = (r - 1) * rows + row
        return pltpu.make_async_remote_copy(
            src_ref=part.at[at], dst_ref=recv.at[at],
            send_sem=part_send.at[at], recv_sem=part_recv.at[at],
            device_id=layer_id(r), device_id_type=MESH,
        )

    barrier = pltpu.get_barrier_semaphore()
    for by in (-2, -1, 1, 2):
        pl.semaphore_signal(barrier, inc=1, device_id=group_id(by), device_id_type=MESH)
    for r in range(1, layers):
        pl.semaphore_signal(barrier, inc=1, device_id=layer_id(r), device_id_type=MESH)
    pl.semaphore_wait(barrier, 4 + layers - 1)

    for q in range(steps):
        count = halo_count(q)
        for by in (1, 2):
            column = base + q * layers + layer - by * rows

            def send(t, carry, q=q, by=by, column=column):
                row = t - (by - 1) * rows
                slot, hit = find(row, column)
                block = vals_ref[row, slot]
                pack[q * far + t] = jnp.where(hit > 0, block, jnp.zeros_like(block))
                halo_copy(q, t, by).start()
                return carry

            lax.fori_loop((by - 1) * rows, jnp.clip(count, (by - 1) * rows, by * rows), send, 0)

    right[zero_at] = jnp.zeros(right.shape[1:], right.dtype)

    def keep(n, carry):
        right[n] = vals_ref[n // slots, n % slots]
        return carry

    lax.fori_loop(0, rows * slots, keep, 0)

    def product(row, o):
        target = targets_ref[row, o]
        there = target - base
        near = jnp.clip(there, 0, rows - 1)
        total = None
        for s in range(slots):
            column = cols_ref[row, s]
            slot, hit = find(near, column)
            local_at = jnp.where(hit > 0, near * slots + slot, zero_at)
            t = there - rows
            place = column - base
            q = (place - layer) // layers
            reach = (place >= t + rows - W) & (t < far)
            far_at = jnp.where(reach, halo_at + q * far + t, zero_at)
            at = jnp.where(there < rows, local_at, far_at)
            at = jnp.where((target >= 0) & (column >= 0), at, zero_at)
            at = jnp.clip(at, 0, right.shape[0] - 1)
            term = lax.dot_general(
                vals_ref[row, s], right[at], (((1,), (1,)), ((), ())),
                preferred_element_type=jnp.float32,
            )
            total = term if total is None else total + term
        slot, hit = find(row, target)
        mine = (hit > 0) & (target >= 0)
        block = vals_ref[row, jnp.where(mine, slot, 0)].astype(jnp.float32)
        twice = jnp.where(mine, 2.0 * block, jnp.zeros_like(block))
        return twice - total

    def one_row(row, carry):
        for r in range(1, layers):
            part[(r - 1) * rows + row] = product(row, (layer + r) % layers).astype(part.dtype)
            part_copy(row, r).start()
        own[row] = product(row, layer)
        return carry

    for q in range(steps):
        count = halo_count(q)

        def arrive(t, carry, q=q):
            halo_copy(q, t, 1).wait_recv()
            right[halo_at + q * far + t] = halo[q * far + t]
            return carry

        lax.fori_loop(0, count, arrive, 0)
        first = jnp.clip(q * layers + layer - W, 0, rows) if q else 0
        last = jnp.clip((q + 1) * layers + layer - W, 0, rows) if q < steps - 1 else rows
        lax.fori_loop(first, last, one_row, 0)

    def finish(row, carry):
        total = own[row]
        for r in range(1, layers):
            part_copy(row, r).wait_recv()
            total = total + recv[(r - 1) * rows + row].astype(jnp.float32)
        out_ref[row, 0] = total.astype(out_ref.dtype)
        return carry

    lax.fori_loop(0, rows, finish, 0)

    for q in range(steps):
        lax.fori_loop(0, halo_count(q), lambda t, c, q=q: (halo_copy(q, t, 1).wait_send(), c)[1], 0)
    for r in range(1, layers):
        lax.fori_loop(0, rows, lambda row, c, r=r: (part_copy(row, r).wait_send(), c)[1], 0)


def solution(mesh):
    layers = mesh.shape["layer"]
    fine = mesh.shape["col"]
    groups = mesh.shape["row"] * fine

    def per_device(cols, vals, outcols):
        rows, slots, size, _ = vals.shape
        outs = outcols.shape[1]
        far = 2 * W
        steps = -(-(rows + W) // layers)
        block = (size, size)
        sent = (layers - 1) * rows
        return pl.pallas_call(
            functools.partial(kernel, (rows, slots, outs, layers, groups, fine)),
            out_shape=jax.ShapeDtypeStruct((rows, outs // layers) + block, jnp.bfloat16),
            in_specs=[
                pl.BlockSpec(memory_space=pltpu.SMEM),
                pl.BlockSpec(memory_space=pltpu.SMEM),
                pl.BlockSpec(memory_space=pltpu.VMEM),
            ],
            out_specs=pl.BlockSpec(memory_space=pltpu.VMEM),
            scratch_shapes=[
                pltpu.VMEM((steps * far,) + block, jnp.bfloat16),
                pltpu.VMEM((steps * far,) + block, jnp.bfloat16),
                pltpu.VMEM((rows * slots + 1 + steps * far,) + block, jnp.bfloat16),
                pltpu.VMEM((sent,) + block, jnp.bfloat16),
                pltpu.VMEM((rows,) + block, jnp.float32),
                pltpu.VMEM((sent,) + block, jnp.bfloat16),
                pltpu.SemaphoreType.DMA((steps * far,)),
                pltpu.SemaphoreType.DMA((steps * far,)),
                pltpu.SemaphoreType.DMA((sent,)),
                pltpu.SemaphoreType.DMA((sent,)),
            ],
            compiler_params=pltpu.CompilerParams(collective_id=0, has_side_effects=True),
        )(cols, outcols, vals)

    in_specs = (
        P(("row", "col"), "layer"),
        P(("row", "col"), "layer", None, None),
        P(("row", "col"), None),
    )
    return jax.shard_map(
        per_device, mesh=mesh, in_specs=in_specs,
        out_specs=P(("row", "col"), "layer", None, None), check_vma=False,
    )
```

time: 374 us -> 102 us (0.27)
  waiting for transfers between devices: 249 us -> 0 us
  Pallas kernels: 0 us -> 97 us
  local copies, waits for them, and re-layouts: 67.6 us -> 4.95 us
  matrix products: 25.5 us -> 0 us
  between operations: 13.5 us -> 0.01 us
  other arithmetic: 11.3 us -> 0 us
  starting transfers between devices: 5.27 us -> 0 us
    ppermute x4 -> x0, waiting for transfers between devices: 145 us -> none  [passed_along(): return lax.ppermute(value, axis, pairs)]
    psum x1 -> x0, waiting for transfers between devices: 104 us -> none  [per_device(): total = lax.psum(partials.astype(jnp.bfloat16), 'layer').astype(jnp.float32)]
    pallas_call x0 -> x1, Pallas kernels: none -> 97 us  [per_device(): pl.pallas_call(functools.partial(kernel, (rows, slots, outs, layers, grou...]
    gather x16 -> x0, local copies, waits for them, and re-layouts: 41.8 us -> none  [the longest x8 37.3 us: one_row(): right = extended[where]]
    dot_general x24 -> x0, matrix products: 25.5 us -> none  [the longest x8 14.1 us: one_row(): jnp.einsum('ost,otab->osab', hits, right, preferred_element_type=jnp.floa...]
    dynamic_slice x16 -> x0, local copies, waits for them, and re-layouts: 11.9 us -> none  [per_device(): partials = lax.map(one_row, (vals, cols, outcols))]
    concatenate x2 -> x0, other arithmetic: 8.83 us -> none  [the longest x1 8.76 us: per_device(): extended = jnp.concatenate(blocks_list, axis=0)]
    dynamic_update_slice x8 -> x0, local copies, waits for them, and re-layouts: 7 us -> none  [per_device(): partials = lax.map(one_row, (vals, cols, outcols))]
  transfers between devices with their start and end apart: 5 -> 0, of which waited for: 4 -> 0; matrix products, arithmetic and copies ran while one was open for 0% -> 0% of each run, Pallas kernels for 0% -> 0%
where the time goes in v1:
time: 102 us
  Pallas kernels  97 us (95%)
  local copies, waits for them, and re-layouts  4.95 us (5%)
    pallas_call x1, Pallas kernels, per_device(): pl.pallas_call(functools.partial(kernel, (rows, slots, outs, layers, grou...  97 us
    unnamed x3, local copies, waits for them, and re-layouts  4.95 us

profile of v1, /device:TPU:0, one launch (start us, length us, event | category | flops | bytes accessed | tf_op | source)
XLA Modules:
  0.0 102.0 jit_solution(4206839821282639292)
XLA Ops:
  0.0 1.3 %copy.4.cols_ref = s32[8,4]{1,0:T(8,128)} copy(s32[8,4]{0,1:T(4,128)} %param.3) | data formatting | bytes 256 | tf_op args[0]
  1.3 1.3 %copy.5.targets_ref = s32[8,4]{1,0:T(8,128)} copy(s32[8,4]{0,1:T(4,128)} %param.5) | data formatting | bytes 256 | tf_op args[2]
  2.7 97.0 %shard_map.37 = bf16[8,1,256,256]{3,2,1,0:T(8,128)(2,1)} custom-call(s32[8,4]{1,0:T(8,128)} %copy.4.cols_ref, s32[8,4]{1,0:T(8,128)} %copy.5.targets_ref, bf16[8,4,256,256]{3,2,1,0:T(8,128)(2,1)} %vals_ref.1), custom_call_target="tpu_custom_call" | custom-call | tf_op jit(solution)/shard_map/pallas_call | solution.py:170
  99.7 2.3 %copy.7 = bf16[8,1,256,256]{3,2,1,0:T(8,128)(2,1)} copy(bf16[8,1,256,256]{3,2,1,0:T(8,128)(2,1)} %shard_map.37) | data formatting | bytes 2097152
